TPU v7x, 128 devices: a whole 4x4x4 slice. The times are simulated.
128 devices in a mesh: gx: 4 (over x), gy: 32 (over y, z, core).
Axes of the slice: x: 4, y: 4, z: 4, core: 2. Of those that a mesh axis runs over, the one named last changes fastest.
Arguments:
- charge: float32 [192, 256, 128], P('gx', 'gy'), may hold values from -6 to 6
- kernel_fine: float32 [11, 11, 11], replicated, may hold values from -0.15625 to 0.15625
- kernel_mid: float32 [11, 11, 11], replicated, may hold values from -0.125 to 0.125
- kernel_top: float32 [11, 11, 11], replicated, may hold values from -0.0625 to 0.0625
Outputs:
- potential: float32 [192, 256, 128], P('gx', 'gy')
All inputs are finite; a program needn't handle non-finite values.
Results may differ from a plain program's by a relative error of at most 0.000073.
Values sent between devices are 32-bit elements; how exact they have to be, the bound alone decides.
A program may use at most 128 MiB of HBM per device.

v0:
```python
import jax
import jax.numpy as jnp
from jax import lax
from jax.sharding import PartitionSpec as P

SPLINE = (0.125, 0.5, 0.75, 0.5, 0.125)
HIGHEST = lax.Precision.HIGHEST


def with_halo(cells, sides, width):
    for axis, dim in sides:
        count = lax.axis_size(axis)
        ends = count - 1
        head = lax.slice_in_dim(cells, 0, width, axis=dim)
        tail = lax.slice_in_dim(cells, cells.shape[dim] - width, cells.shape[dim], axis=dim)
        cells = jnp.concatenate(
            [
                lax.ppermute(tail, axis, [(i, (i + 1) % count) for i in range(ends)]),
                cells,
                lax.ppermute(head, axis, [((i + 1) % count, i) for i in range(ends)]),
            ],
            axis=dim,
        )
    return cells


def from_behind(value, axis, steps):
    count = lax.axis_size(axis)
    leading, last = (max(0, -steps), min(count, count - steps))
    return lax.ppermute(value, axis, [(source, source + steps) for source in range(leading, last)])


def slab_faces(block, width):
    return with_halo(block, (("gx", 0),), width)


def neighbour_rows(piece, distance):
    return from_behind(piece, "gy", distance)


def top_neighbour_rows(piece, distance):
    return from_behind(piece, "gy", distance)


def row_hops(slab, width, mover):
    rows = slab.shape[1]
    lower = []
    upper = []
    reach = 0
    distance = 1
    while reach < width:
        count = min(rows, width - reach)
        lower.insert(0, mover(slab[:, rows - count :], distance))
        upper.append(mover(slab[:, :count], -distance))
        reach = reach + count
        distance = distance + 1
    return jnp.concatenate(lower + [slab] + upper, axis=1)


def fine_rims(block, width):
    return row_hops(slab_faces(block, width), width, neighbour_rows)


def coarse_rims(block, width):
    slab = slab_faces(block, width)
    return row_hops(slab, width, neighbour_rows)


def edge_mask(count_x, count_y, rim):
    places_x = lax.axis_index("gx") * count_x - rim + jnp.arange(count_x + 2 * rim)
    places_y = lax.axis_index("gy") * count_y - rim + jnp.arange(count_y + 2 * rim)
    inside_x = ((places_x >= 0) & (places_x < lax.axis_size("gx") * count_x)).astype(jnp.float32)
    inside_y = ((places_y >= 0) & (places_y < lax.axis_size("gy") * count_y)).astype(jnp.float32)
    return inside_x[:, None, None] * inside_y[None, :, None]


def band_matrices(kernel, block_len):
    span = kernel.shape[2]
    window = block_len + span - 1
    offset = jnp.arange(window)[:, None] - jnp.arange(block_len)[None, :]
    onehot = (offset[:, :, None] == jnp.arange(span)[None, None, :]).astype(jnp.float32)
    return jnp.einsum("abc,stc->abst", kernel, onehot, precision=HIGHEST)


def convolve(padded, kernel):
    span = kernel.shape[0]
    radius = span // 2
    width_x = padded.shape[0] - 2 * radius
    full_y = padded.shape[1]
    width_y = full_y - 2 * radius
    length = padded.shape[2]
    block_len = min(128, length)
    blocks = length // block_len
    window = block_len + span - 1
    deeper = jnp.pad(padded, ((0, 0), (0, 0), (radius, radius)))
    framed = jnp.stack([deeper], axis=2)
    matrices = (
        band_matrices(kernel, block_len)
        .transpose(0, 2, 1, 3)
        .reshape(span, window, span * block_len)
    )

    def add_plane(plane_index, total):
        plane = lax.dynamic_slice_in_dim(framed, plane_index, width_x, 0)
        weights = lax.dynamic_index_in_dim(matrices, plane_index, 0, keepdims=False)
        product = jnp.dot(
            plane.reshape(-1, window),
            weights,
            precision=HIGHEST,
            preferred_element_type=jnp.float32,
        )
        product = product.reshape(width_x, full_y, blocks, span, block_len)
        for offset in range(span):
            total = total + product[:, offset : offset + width_y, :, offset, :]
        return total

    start_total = jnp.zeros((width_x, width_y, blocks, block_len), jnp.float32)
    total = lax.fori_loop(0, span, add_plane, start_total)
    return total.reshape(width_x, width_y, length)


def restrict_axis(values, axis, rim):
    half = (values.shape[axis] - 2 * rim) // 2
    total = None
    for place, weight in enumerate(SPLINE):
        start = rim - 2 + place
        piece = lax.slice_in_dim(values, start, start + 2 * half - 1, 2, axis)
        total = weight * piece if total is None else total + weight * piece
    return total


def restrict_block(padded, rim):
    along_x = restrict_axis(padded, 0, rim)
    along_y = restrict_axis(along_x, 1, rim)
    deeper = jnp.pad(along_y, ((0, 0), (0, 0), (2, 2)))
    return restrict_axis(deeper, 2, 2)


def prolong_axis(values, axis):
    count = values.shape[axis] - 2
    before = lax.slice_in_dim(values, 0, count, 1, axis)
    centre = lax.slice_in_dim(values, 1, count + 1, 1, axis)
    after = lax.slice_in_dim(values, 2, count + 2, 1, axis)
    even = 0.125 * before + 0.75 * centre + 0.125 * after
    odd = 0.5 * centre + 0.5 * after
    target = list(values.shape)
    target[axis] = 2 * count
    return jnp.stack([even, odd], axis=axis + 1).reshape(target)


def prolong_window(framed):
    values = jnp.pad(framed, ((0, 0), (0, 0), (1, 1)))
    for axis in range(3):
        values = prolong_axis(values, axis)
    return values


def top_level(top_block, kernel_top, radius, cycle):
    size_x, size_y, depth = top_block.shape
    reach = radius + cycle
    slab = with_halo(top_block, (("gx", 0),), reach)
    framed = row_hops(slab, reach, top_neighbour_rows)
    result = convolve(framed, kernel_top)
    return result * edge_mask(size_x, size_y, cycle)


def shards(charge, kernel_fine, kernel_mid, kernel_top):
    radius = kernel_fine.shape[0] // 2
    cycle = 1
    middle_rim = radius + cycle - 1
    fine_padded = fine_rims(charge, radius)
    middle_charge = restrict_block(fine_padded, radius)
    middle_padded = coarse_rims(middle_charge, middle_rim)
    top_block = restrict_block(middle_padded, middle_rim)
    top_window = top_level(top_block, kernel_top, radius, cycle)
    middle_conv = convolve(middle_padded, kernel_mid)
    middle_potential = middle_conv + prolong_window(top_window)
    middle_window = with_halo(middle_potential, (("gx", 0), ("gy", 1)), 1)
    return convolve(fine_padded, kernel_fine) + prolong_window(middle_window)


def solution(mesh):
    placed = (P("gx", "gy", None), P(), P(), P())
    return jax.shard_map(
        shards, mesh=mesh, in_specs=placed, out_specs=P("gx", "gy", None), check_vma=False
    )
```

profile of v0, /device:TPU:26, one launch (start us, length us, event | category | flops | bytes accessed | tf_op | source)
XLA Modules:
  0.0 318.8 jit_solution(14307604880468959349)
XLA Ops:
  6.7 5.8 %convolution_bitcast_fusion.4 = f32[11,74,11,64]{1,2,0,3:T(8,128)} fusion(s32[74,64]{0,1:T(8,128)S(1)} %iota_subtract_fusion.1, f32[11,11,11]{2,1,0:T(8,128)} %param.12), kind=kOutput, calls=%fused_computation.85 | convolution fusion | flops 75695488 | bytes 2316492 | tf_op jit(solution)/shard_map/abc,stc->abst/dot_general | solution.py:82
  12.5 7.8 %convolution_bitcast_fusion.3 = f32[11,138,11,128]{3,2,0,1:T(8,128)} fusion(s32[138,128]{1,0:T(8,128)S(1)} %iota_subtract_fusion, f32[11,11,11]{2,1,0:T(8,128)S(1)} %copy-done), kind=kOutput, calls=%fused_computation.84 | convolution fusion | flops 282323712 | bytes 8625356 | tf_op jit(solution)/shard_map/abc,stc->abst/dot_general | solution.py:82
  22.3 5.9 %collective-permute-start.3 = (f32[58,5,128]{2,1,0:T(8,128)S(1)}, f32[58,5,128]{2,1,0:T(8,128)S(1)}, u32[]{:S(2)}, u32[]{:S(2)}) collective-permute-start(f32[58,5,128]{2,1,0:T(8,128)S(1)} %get-tuple-element.355), channel_id=1, source_target_pairs={{1,0},{2,1},{3,2},{4,3},{5,4},{6,5},{7,6},{8,7},{9,8},{10,9},{11,1... | collective-permute-start | bytes 445448 | tf_op jit(solution)/shard_map/ppermute | solution.py:30
  47.8 5.8 %collective-permute-start.8 = (f32[34,4,64]{2,1,0:T(4,128)S(1)}, f32[34,4,64]{2,1,0:T(4,128)S(1)}, u32[]{:S(2)}, u32[]{:S(2)}) collective-permute-start(f32[34,4,64]{2,1,0:T(4,128)S(1)} %pad_maximum_fusion.5), channel_id=1, source_target_pairs={{1,0},{2,1},{3,2},{4,3},{5,4},{6,5},{7,6},{8,7},{9,8},{10,9},{11,1... | collective-permute-start | bytes 104456 | tf_op jit(solution)/shard_map/ppermute | solution.py:30
  55.6 6.0 %collective-permute-start.9 = (f32[34,1,64]{2,1,0:T(1,128)S(1)}, f32[34,1,64]{2,1,0:T(1,128)S(1)}, u32[]{:S(2)}, u32[]{:S(2)}) collective-permute-start(f32[34,1,64]{2,1,0:T(1,128)S(1)} %get-tuple-element.366), channel_id=1, source_target_pairs={{2,0},{3,1},{4,2},{5,3},{6,4},{7,5},{8,6},{9,7},{10,8},{11,9},{12,... | collective-permute-start | bytes 26120 | tf_op jit(solution)/shard_map/ppermute | solution.py:30
  70.7 5.9 %copy.221 = f32[11,74,11,64]{1,3,2,0:T(8,128)} copy(f32[11,74,11,64]{1,2,0,3:T(8,128)} %convolution_bitcast_fusion.4) | data formatting | bytes 4584448 | tf_op jit(solution)/shard_map/transpose | solution.py:99
  78.5 13.6 %reshape.207 = f32[11,138,1408]{2,0,1:T(8,128)} reshape(f32[11,138,11,128]{3,2,0,1:T(8,128)} %convolution_bitcast_fusion.3) | data formatting | bytes 17098752 | tf_op jit(solution)/shard_map/reshape | solution.py:100
  98.2 5.8 %collective-permute-start.15 = (f32[24,2,32]{2,1,0:T(2,128)S(1)}, f32[24,2,32]{2,1,0:T(2,128)S(1)}, u32[]{:S(2)}, u32[]{:S(2)}) collective-permute-start(f32[24,2,32]{2,1,0:T(2,128)S(1)} %pad_maximum_fusion.8), channel_id=1, source_target_pairs={{1,0},{2,1},{3,2},{4,3},{5,4},{6,5},{7,6},{8,7},{9,8},{10,9},{11,1... | collective-permute-start | bytes 18440 | tf_op jit(solution)/shard_map/ppermute | solution.py:30
  103.9 4.2 %collective-permute-start.16 = (f32[24,2,32]{2,1,0:T(2,128)S(1)}, f32[24,2,32]{2,1,0:T(2,128)S(1)}, u32[]{:S(2)}, u32[]{:S(2)}) collective-permute-start(f32[24,2,32]{2,1,0:T(2,128)S(1)} %pad_maximum_fusion.8), channel_id=1, source_target_pairs={{2,0},{3,1},{4,2},{5,3},{6,4},{7,5},{8,6},{9,7},{10,8},{11,9},{12,... | collective-permute-start | bytes 18440 | tf_op jit(solution)/shard_map/ppermute | solution.py:30
  111.5 30.6 %while.43 = (s32[]{:T(128)}, f32[24,4,1,64]{3,0,1,2:T(8,128)S(1)}, f32[34,14,1,74]{3,0,1,2:T(8,128)S(1)}, f32[11,74,704]{1,2,0:T(8,128)}, s32[]{:T(128)}, /*index=5*/s32[]{:T(128)}) while((s32[]{:T(128)}, f32[24,4,1,64]{3,0,1,2:T(8,128)S(1)}, f32[34,14,1,74]{3,0,1,2:T(8,128)S(1)}, f32[11,74,704]{1,2,0:T(8,128)}, s32[]{:T(128)}, ...), condition=%wide.region_3.4_spmd.clone, body=%wide.region_2.3_spmd.clone.sunk | while | flops 210124800 | bytes 2214999 | solution.py:118
  143.2 24.6 %while.44 = (s32[]{:T(128)}, f32[14,4,1,32]{3,1,0,2:T(4,128)S(1)}, f32[24,14,1,42]{3,1,0,2:T(8,128)S(1)}, f32[11,42,352]{1,2,0:T(8,128)}, s32[]{:T(128)}, /*index=5*/s32[]{:T(128)}) while((s32[]{:T(128)}, f32[14,4,1,32]{3,1,0,2:T(4,128)S(1)}, f32[24,14,1,42]{3,1,0,2:T(8,128)S(1)}, f32[11,42,352]{1,2,0:T(8,128)}, s32[]{:T(128)}, ...), condition=%wide.region_5.6_spmd.clone, body=%wide.region_4.5_spmd.clone.sunk | while | flops 34793472 | bytes 782423 | solution.py:118
  181.7 5.8 %collective-permute-start.21 = (f32[26,1,64]{2,1,0:T(1,128)S(1)}, f32[26,1,64]{2,1,0:T(1,128)S(1)}, u32[]{:S(2)}, u32[]{:S(2)}) collective-permute-start(f32[26,1,64]{2,1,0:T(1,128)S(1)} %get-tuple-element.369), channel_id=1, source_target_pairs={{1,0},{2,1},{3,2},{4,3},{5,4},{6,5},{7,6},{8,7},{9,8},{10,9},{11,1... | collective-permute-start | bytes 19976 | tf_op jit(solution)/shard_map/ppermute | solution.py:20
  187.5 129.2 %while.42 = (s32[]{:T(128)}, f32[48,8,1,128]{3,0,1,2:T(8,128)S(1)}, f32[58,18,1,138]{3,0,1,2:T(8,128)S(1)}, f32[11,138,1408]{2,0,1:T(8,128)}, s32[]{:T(128)}, /*index=5*/s32[]{:T(128)}) while((s32[]{:T(128)}, f32[48,8,1,128]{3,0,1,2:T(8,128)S(1)}, f32[58,18,1,138]{3,0,1,2:T(8,128)S(1)}, f32[11,138,1408]{2,0,1:T(8,128)}, s32[]{:T(128)}, ...), condition=%wide.region_1.2_spmd.clone, body=%wide.region_0.1_spmd.clone.sunk | while | flops 2015133696 | bytes 14100567 | solution.py:118
  191.0 6.3 %convolution_bitcast_fusion.9 = f32[48,18,1,11,128]{4,0,3,1,2:T(8,128)} fusion(f32[58,18,1,138]{3,0,1,2:T(8,128)S(1)} %get-tuple-element.505, s32[]{:T(128)} %get-tuple-element.497, f32[11,128,138]{1,0,2:T(8,128)S(1)} %reshape.209), kind=kOutput, calls=%fused_computation.clone.1 | convolution fusion | flops 2014543872 | bytes 6881284 | tf_op jit(solution)/shard_map/while/body/eval_jaxpr/dot_general | solution.py:106
  202.8 6.3 %convolution_bitcast_fusion.9 = f32[48,18,1,11,128]{4,0,3,1,2:T(8,128)} fusion(f32[58,18,1,138]{3,0,1,2:T(8,128)S(1)} %get-tuple-element.505, s32[]{:T(128)} %get-tuple-element.497, f32[11,128,138]{1,0,2:T(8,128)S(1)} %reshape.209), kind=kOutput, calls=%fused_computation.clone.1 | convolution fusion | flops 2014543872 | bytes 6881284 | tf_op jit(solution)/shard_map/while/body/eval_jaxpr/dot_general | solution.py:106
  214.6 6.3 %convolution_bitcast_fusion.9 = f32[48,18,1,11,128]{4,0,3,1,2:T(8,128)} fusion(f32[58,18,1,138]{3,0,1,2:T(8,128)S(1)} %get-tuple-element.505, s32[]{:T(128)} %get-tuple-element.497, f32[11,128,138]{1,0,2:T(8,128)S(1)} %reshape.209), kind=kOutput, calls=%fused_computation.clone.1 | convolution fusion | flops 2014543872 | bytes 6881284 | tf_op jit(solution)/shard_map/while/body/eval_jaxpr/dot_general | solution.py:106
  226.3 6.3 %convolution_bitcast_fusion.9 = f32[48,18,1,11,128]{4,0,3,1,2:T(8,128)} fusion(f32[58,18,1,138]{3,0,1,2:T(8,128)S(1)} %get-tuple-element.505, s32[]{:T(128)} %get-tuple-element.497, f32[11,128,138]{1,0,2:T(8,128)S(1)} %reshape.209), kind=kOutput, calls=%fused_computation.clone.1 | convolution fusion | flops 2014543872 | bytes 6881284 | tf_op jit(solution)/shard_map/while/body/eval_jaxpr/dot_general | solution.py:106
  238.1 6.3 %convolution_bitcast_fusion.9 = f32[48,18,1,11,128]{4,0,3,1,2:T(8,128)} fusion(f32[58,18,1,138]{3,0,1,2:T(8,128)S(1)} %get-tuple-element.505, s32[]{:T(128)} %get-tuple-element.497, f32[11,128,138]{1,0,2:T(8,128)S(1)} %reshape.209), kind=kOutput, calls=%fused_computation.clone.1 | convolution fusion | flops 2014543872 | bytes 6881284 | tf_op jit(solution)/shard_map/while/body/eval_jaxpr/dot_general | solution.py:106
  249.8 6.3 %convolution_bitcast_fusion.9 = f32[48,18,1,11,128]{4,0,3,1,2:T(8,128)} fusion(f32[58,18,1,138]{3,0,1,2:T(8,128)S(1)} %get-tuple-element.505, s32[]{:T(128)} %get-tuple-element.497, f32[11,128,138]{1,0,2:T(8,128)S(1)} %reshape.209), kind=kOutput, calls=%fused_computation.clone.1 | convolution fusion | flops 2014543872 | bytes 6881284 | tf_op jit(solution)/shard_map/while/body/eval_jaxpr/dot_general | solution.py:106
  261.6 6.3 %convolution_bitcast_fusion.9 = f32[48,18,1,11,128]{4,0,3,1,2:T(8,128)} fusion(f32[58,18,1,138]{3,0,1,2:T(8,128)S(1)} %get-tuple-element.505, s32[]{:T(128)} %get-tuple-element.497, f32[11,128,138]{1,0,2:T(8,128)S(1)} %reshape.209), kind=kOutput, calls=%fused_computation.clone.1 | convolution fusion | flops 2014543872 | bytes 6881284 | tf_op jit(solution)/shard_map/while/body/eval_jaxpr/dot_general | solution.py:106
  273.4 6.3 %convolution_bitcast_fusion.9 = f32[48,18,1,11,128]{4,0,3,1,2:T(8,128)} fusion(f32[58,18,1,138]{3,0,1,2:T(8,128)S(1)} %get-tuple-element.505, s32[]{:T(128)} %get-tuple-element.497, f32[11,128,138]{1,0,2:T(8,128)S(1)} %reshape.209), kind=kOutput, calls=%fused_computation.clone.1 | convolution fusion | flops 2014543872 | bytes 6881284 | tf_op jit(solution)/shard_map/while/body/eval_jaxpr/dot_general | solution.py:106
  285.1 6.3 %convolution_bitcast_fusion.9 = f32[48,18,1,11,128]{4,0,3,1,2:T(8,128)} fusion(f32[58,18,1,138]{3,0,1,2:T(8,128)S(1)} %get-tuple-element.505, s32[]{:T(128)} %get-tuple-element.497, f32[11,128,138]{1,0,2:T(8,128)S(1)} %reshape.209), kind=kOutput, calls=%fused_computation.clone.1 | convolution fusion | flops 2014543872 | bytes 6881284 | tf_op jit(solution)/shard_map/while/body/eval_jaxpr/dot_general | solution.py:106
  296.8 6.3 %convolution_bitcast_fusion.9 = f32[48,18,1,11,128]{4,0,3,1,2:T(8,128)} fusion(f32[58,18,1,138]{3,0,1,2:T(8,128)S(1)} %get-tuple-element.505, s32[]{:T(128)} %get-tuple-element.497, f32[11,128,138]{1,0,2:T(8,128)S(1)} %reshape.209), kind=kOutput, calls=%fused_computation.clone.1 | convolution fusion | flops 2014543872 | bytes 6881284 | tf_op jit(solution)/shard_map/while/body/eval_jaxpr/dot_general | solution.py:106
  308.5 6.3 %convolution_bitcast_fusion.9 = f32[48,18,1,11,128]{4,0,3,1,2:T(8,128)} fusion(f32[58,18,1,138]{3,0,1,2:T(8,128)S(1)} %get-tuple-element.505, s32[]{:T(128)} %get-tuple-element.497, f32[11,128,138]{1,0,2:T(8,128)S(1)} %reshape.209), kind=kOutput, calls=%fused_computation.clone.1 | convolution fusion | flops 2014543872 | bytes 6881284 | tf_op jit(solution)/shard_map/while/body/eval_jaxpr/dot_general | solution.py:106
  (243 shorter events, 180.9 us)
Async XLA Ops:
  0.0 12.5 %copy-start = (f32[11,11,11]{2,1,0:T(8,128)S(1)}, f32[11,11,11]{2,1,0:T(8,128)}, u32[]{:S(2)}) copy-start(f32[11,11,11]{2,1,0:T(8,128)} %param.11) | copy-start | bytes 15976
  0.8 19.5 %collective-permute-start = (f32[5,8,128]{2,1,0:T(8,128)S(1)}, f32[5,8,128]{2,1,0:T(8,128)S(1)}, u32[]{:S(2)}, u32[]{:S(2)}) collective-permute-start(f32[5,8,128]{2,1,0:T(8,128)S(1)} %get-tuple-element.359), channel_id=1, source_target_pairs={{0,32},{32,64},{64,96},{1,33},{33,65},{65,97},{2,34},{34,66},{66,9... | collective-permute-start | bytes 61448 | tf_op jit(solution)/shard_map/ppermute | solution.py:18
  4.2 16.2 %collective-permute-start.1 = (f32[5,8,128]{2,1,0:T(8,128)S(1)}, f32[5,8,128]{2,1,0:T(8,128)S(1)}, u32[]{:S(2)}, u32[]{:S(2)}) collective-permute-start(f32[5,8,128]{2,1,0:T(8,128)S(1)} %get-tuple-element.358), channel_id=1, source_target_pairs={{32,0},{64,32},{96,64},{33,1},{65,33},{97,65},{34,2},{66,34},{98,6... | collective-permute-start | bytes 61448 | tf_op jit(solution)/shard_map/ppermute | solution.py:20
  12.5 15.8 %copy-start.3 = (f32[11,11,11]{2,1,0:T(8,128)S(1)}, f32[11,11,11]{2,1,0:T(8,128)}, u32[]{:S(2)}) copy-start(f32[11,11,11]{2,1,0:T(8,128)} %param.13) | copy-start | bytes 15976
  20.4 10.8 %collective-permute-start.2 = (f32[58,5,128]{2,1,0:T(8,128)S(1)}, f32[58,5,128]{2,1,0:T(8,128)S(1)}, u32[]{:S(2)}, u32[]{:S(2)}) collective-permute-start(f32[58,5,128]{2,1,0:T(8,128)S(1)} %get-tuple-element.354), channel_id=1, source_target_pairs={{0,1},{1,2},{2,3},{3,4},{4,5},{5,6},{6,7},{7,8},{8,9},{9,10},{10,1... | collective-permute-start | bytes 445448 | tf_op jit(solution)/shard_map/ppermute | solution.py:30
  22.3 9.4 %collective-permute-start.3 = (f32[58,5,128]{2,1,0:T(8,128)S(1)}, f32[58,5,128]{2,1,0:T(8,128)S(1)}, u32[]{:S(2)}, u32[]{:S(2)}) collective-permute-start(f32[58,5,128]{2,1,0:T(8,128)S(1)} %get-tuple-element.355), channel_id=1, source_target_pairs={{1,0},{2,1},{3,2},{4,3},{5,4},{6,5},{7,6},{8,7},{9,8},{10,9},{11,1... | collective-permute-start | bytes 445448 | tf_op jit(solution)/shard_map/ppermute | solution.py:30
  36.9 5.9 %collective-permute-start.4 = (f32[5,4,64]{2,1,0:T(4,128)S(1)}, f32[5,4,64]{2,1,0:T(4,128)S(1)}, u32[]{:S(2)}, u32[]{:S(2)}) collective-permute-start(f32[5,4,64]{2,1,0:T(4,128)S(1)} %get-tuple-element.374), channel_id=1, source_target_pairs={{0,32},{32,64},{64,96},{1,33},{33,65},{65,97},{2,34},{34,66},{66,9... | collective-permute-start | bytes 15368 | tf_op jit(solution)/shard_map/ppermute | solution.py:18
  40.3 5.6 %collective-permute-start.5 = (f32[5,4,64]{2,1,0:T(4,128)S(1)}, f32[5,4,64]{2,1,0:T(4,128)S(1)}, u32[]{:S(2)}, u32[]{:S(2)}) collective-permute-start(f32[5,4,64]{2,1,0:T(4,128)S(1)} %get-tuple-element.375), channel_id=1, source_target_pairs={{32,0},{64,32},{96,64},{33,1},{65,33},{97,65},{34,2},{66,34},{98,6... | collective-permute-start | bytes 15368 | tf_op jit(solution)/shard_map/ppermute | solution.py:20
  45.9 17.1 %collective-permute-start.7 = (f32[34,4,64]{2,1,0:T(4,128)S(1)}, f32[34,4,64]{2,1,0:T(4,128)S(1)}, u32[]{:S(2)}, u32[]{:S(2)}) collective-permute-start(f32[34,4,64]{2,1,0:T(4,128)S(1)} %pad_maximum_fusion.5), channel_id=1, source_target_pairs={{0,1},{1,2},{2,3},{3,4},{4,5},{5,6},{6,7},{7,8},{8,9},{9,10},{10,1... | collective-permute-start | bytes 104456 | tf_op jit(solution)/shard_map/ppermute | solution.py:30
  47.8 15.2 %collective-permute-start.8 = (f32[34,4,64]{2,1,0:T(4,128)S(1)}, f32[34,4,64]{2,1,0:T(4,128)S(1)}, u32[]{:S(2)}, u32[]{:S(2)}) collective-permute-start(f32[34,4,64]{2,1,0:T(4,128)S(1)} %pad_maximum_fusion.5), channel_id=1, source_target_pairs={{1,0},{2,1},{3,2},{4,3},{5,4},{6,5},{7,6},{8,7},{9,8},{10,9},{11,1... | collective-permute-start | bytes 104456 | tf_op jit(solution)/shard_map/ppermute | solution.py:30
  53.6 8.0 %collective-permute-start.6 = (f32[34,1,64]{2,1,0:T(1,128)S(1)}, f32[34,1,64]{2,1,0:T(1,128)S(1)}, u32[]{:S(2)}, u32[]{:S(2)}) collective-permute-start(f32[34,1,64]{2,1,0:T(1,128)S(1)} %get-tuple-element.367), channel_id=1, source_target_pairs={{0,2},{1,3},{2,4},{3,5},{4,6},{5,7},{6,8},{7,9},{8,10},{9,11},{10,... | collective-permute-start | bytes 26120 | tf_op jit(solution)/shard_map/ppermute | solution.py:30
  55.6 7.5 %collective-permute-start.9 = (f32[34,1,64]{2,1,0:T(1,128)S(1)}, f32[34,1,64]{2,1,0:T(1,128)S(1)}, u32[]{:S(2)}, u32[]{:S(2)}) collective-permute-start(f32[34,1,64]{2,1,0:T(1,128)S(1)} %get-tuple-element.366), channel_id=1, source_target_pairs={{2,0},{3,1},{4,2},{5,3},{6,4},{7,5},{8,6},{9,7},{10,8},{11,9},{12,... | collective-permute-start | bytes 26120 | tf_op jit(solution)/shard_map/ppermute | solution.py:30
  64.8 27.3 %collective-permute-start.10 = (f32[6,2,32]{2,1,0:T(2,128)S(1)}, f32[6,2,32]{2,1,0:T(2,128)S(1)}, u32[]{:S(2)}, u32[]{:S(2)}) collective-permute-start(f32[6,2,32]{2,1,0:T(2,128)S(1)} %get-tuple-element.378), channel_id=1, source_target_pairs={{0,32},{32,64},{64,96},{1,33},{33,65},{65,97},{2,34},{34,66},{66,9... | collective-permute-start | bytes 4616 | tf_op jit(solution)/shard_map/ppermute | solution.py:18
  67.9 24.2 %collective-permute-start.11 = (f32[6,2,32]{2,1,0:T(2,128)S(1)}, f32[6,2,32]{2,1,0:T(2,128)S(1)}, u32[]{:S(2)}, u32[]{:S(2)}) collective-permute-start(f32[6,2,32]{2,1,0:T(2,128)S(1)} %get-tuple-element.379), channel_id=1, source_target_pairs={{32,0},{64,32},{96,64},{33,1},{65,33},{97,65},{34,2},{66,34},{98,6... | collective-permute-start | bytes 4616 | tf_op jit(solution)/shard_map/ppermute | solution.py:20
  92.2 16.0 %collective-permute-start.12 = (f32[24,2,32]{2,1,0:T(2,128)S(1)}, f32[24,2,32]{2,1,0:T(2,128)S(1)}, u32[]{:S(2)}, u32[]{:S(2)}) collective-permute-start(f32[24,2,32]{2,1,0:T(2,128)S(1)} %pad_maximum_fusion.8), channel_id=1, source_target_pairs={{0,3},{1,4},{2,5},{3,6},{4,7},{5,8},{6,9},{7,10},{8,11},{9,12},{10... | collective-permute-start | bytes 18440 | tf_op jit(solution)/shard_map/ppermute | solution.py:30
  94.3 47.9 %collective-permute-start.13 = (f32[24,2,32]{2,1,0:T(2,128)S(1)}, f32[24,2,32]{2,1,0:T(2,128)S(1)}, u32[]{:S(2)}, u32[]{:S(2)}) collective-permute-start(f32[24,2,32]{2,1,0:T(2,128)S(1)} %pad_maximum_fusion.8), channel_id=1, source_target_pairs={{0,2},{1,3},{2,4},{3,5},{4,6},{5,7},{6,8},{7,9},{8,10},{9,11},{10,... | collective-permute-start | bytes 18440 | tf_op jit(solution)/shard_map/ppermute | solution.py:30
  96.2 46.0 %collective-permute-start.14 = (f32[24,2,32]{2,1,0:T(2,128)S(1)}, f32[24,2,32]{2,1,0:T(2,128)S(1)}, u32[]{:S(2)}, u32[]{:S(2)}) collective-permute-start(f32[24,2,32]{2,1,0:T(2,128)S(1)} %pad_maximum_fusion.8), channel_id=1, source_target_pairs={{0,1},{1,2},{2,3},{3,4},{4,5},{5,6},{6,7},{7,8},{8,9},{9,10},{10,1... | collective-permute-start | bytes 18440 | tf_op jit(solution)/shard_map/ppermute | solution.py:30
  98.2 44.0 %collective-permute-start.15 = (f32[24,2,32]{2,1,0:T(2,128)S(1)}, f32[24,2,32]{2,1,0:T(2,128)S(1)}, u32[]{:S(2)}, u32[]{:S(2)}) collective-permute-start(f32[24,2,32]{2,1,0:T(2,128)S(1)} %pad_maximum_fusion.8), channel_id=1, source_target_pairs={{1,0},{2,1},{3,2},{4,3},{5,4},{6,5},{7,6},{8,7},{9,8},{10,9},{11,1... | collective-permute-start | bytes 18440 | tf_op jit(solution)/shard_map/ppermute | solution.py:30
  103.9 38.3 %collective-permute-start.16 = (f32[24,2,32]{2,1,0:T(2,128)S(1)}, f32[24,2,32]{2,1,0:T(2,128)S(1)}, u32[]{:S(2)}, u32[]{:S(2)}) collective-permute-start(f32[24,2,32]{2,1,0:T(2,128)S(1)} %pad_maximum_fusion.8), channel_id=1, source_target_pairs={{2,0},{3,1},{4,2},{5,3},{6,4},{7,5},{8,6},{9,7},{10,8},{11,9},{12,... | collective-permute-start | bytes 18440 | tf_op jit(solution)/shard_map/ppermute | solution.py:30
  108.2 34.1 %collective-permute-start.17 = (f32[24,2,32]{2,1,0:T(2,128)S(1)}, f32[24,2,32]{2,1,0:T(2,128)}, u32[]{:S(2)}, u32[]{:S(2)}) collective-permute-start(f32[24,2,32]{2,1,0:T(2,128)S(1)} %pad_maximum_fusion.8), channel_id=1, source_target_pairs={{3,0},{4,1},{5,2},{6,3},{7,4},{8,5},{9,6},{10,7},{11,8},{12,9},{13... | collective-permute-start | bytes 18440 | tf_op jit(solution)/shard_map/ppermute | solution.py:30
  168.6 8.2 %collective-permute-start.18 = (f32[1,4,64]{0,2,1:T(8,128)S(1)}, f32[1,4,64]{0,2,1:T(8,128)S(1)}, u32[]{:S(2)}, u32[]{:S(2)}) collective-permute-start(f32[1,4,64]{0,2,1:T(8,128)S(1)} %get-tuple-element.362), channel_id=1, source_target_pairs={{0,32},{32,64},{64,96},{1,33},{33,65},{65,97},{2,34},{34,66},{66,9... | collective-permute-start | bytes 3080 | tf_op jit(solution)/shard_map/ppermute | solution.py:18
  171.7 8.0 %collective-permute-start.19 = (f32[1,4,64]{0,2,1:T(8,128)S(1)}, f32[1,4,64]{0,2,1:T(8,128)S(1)}, u32[]{:S(2)}, u32[]{:S(2)}) collective-permute-start(f32[1,4,64]{0,2,1:T(8,128)S(1)} %get-tuple-element.363), channel_id=1, source_target_pairs={{32,0},{64,32},{96,64},{33,1},{65,33},{97,65},{34,2},{66,34},{98,6... | collective-permute-start | bytes 3080 | tf_op jit(solution)/shard_map/ppermute | solution.py:20
  179.8 137.2 %collective-permute-start.20 = (f32[26,1,64]{2,1,0:T(1,128)S(1)}, f32[26,1,64]{2,1,0:T(1,128)S(1)}, u32[]{:S(2)}, u32[]{:S(2)}) collective-permute-start(f32[26,1,64]{2,1,0:T(1,128)S(1)} %get-tuple-element.368), channel_id=1, source_target_pairs={{0,1},{1,2},{2,3},{3,4},{4,5},{5,6},{6,7},{7,8},{8,9},{9,10},{10,1... | collective-permute-start | bytes 19976 | tf_op jit(solution)/shard_map/ppermute | solution.py:18
  181.7 135.2 %collective-permute-start.21 = (f32[26,1,64]{2,1,0:T(1,128)S(1)}, f32[26,1,64]{2,1,0:T(1,128)S(1)}, u32[]{:S(2)}, u32[]{:S(2)}) collective-permute-start(f32[26,1,64]{2,1,0:T(1,128)S(1)} %get-tuple-element.369), channel_id=1, source_target_pairs={{1,0},{2,1},{3,2},{4,3},{5,4},{6,5},{7,6},{8,7},{9,8},{10,9},{11,1... | collective-permute-start | bytes 19976 | tf_op jit(solution)/shard_map/ppermute | solution.py:20
  (2 other events, 13.7 us)
where the time goes:
time: 322 us; the launch traced here: 319 us
  matrix products  118 us (37%)
  local copies, waits for them, and re-layouts  93.2 us (29%)
  starting transfers between devices  73.5 us (23%)
  other arithmetic  23.2 us (7%)
  waiting for transfers between devices  9.3 us (3%)
    dot_general x33, matrix products, add_plane(): jnp.dot(plane.reshape(-1, window), weights, precision=HIGHEST, preferred_...  101 us
    dynamic_slice x44, local copies, waits for them, and re-layouts, add_plane(): weights = lax.dynamic_index_in_dim(matrices, plane_index, 0, keepdims=False)  58.8 us
    ppermute x12, starting transfers between devices, from_behind(): lax.ppermute(value, axis, [(source, source + steps) for source in range(l...  42.5 us
    add x33, other arithmetic, add_plane(): total = total + product[:, offset:offset + width_y, :, offset, :]  21.8 us
    dot_general x3, matrix products, band_matrices(): return jnp.einsum('abc,stc->abst', kernel, onehot, precision=HIGHEST)  16.5 us
    ppermute x5, starting transfers between devices, with_halo(): lax.ppermute(head, axis, [((i + 1) % count, i) for i in range(ends)])  16.1 us
    ppermute x5, starting transfers between devices, with_halo(): lax.ppermute(tail, axis, [(i, (i + 1) % count) for i in range(ends)])  14.9 us
    reshape x1, local copies, waits for them, and re-layouts, convolve(): matrices = band_matrices(kernel, block_len).transpose(0, 2, 1, 3).reshape...  13.6 us
  transfers between devices with their start and end apart: 22, of which 5 were waited for; matrix products, arithmetic and copies ran while one was open for 62% of the time, Pallas kernels for 0%

commit v1 on v0

v1 whole, which is shorter than its diff:
```python
import functools

import jax
import jax.numpy as jnp
from jax import lax
from jax.experimental import pallas as pl
from jax.experimental.pallas import tpu as pltpu
from jax.sharding import PartitionSpec as P

BF = jnp.bfloat16
F32 = jnp.float32
SPLINE = (0.125, 0.5, 0.75, 0.5, 0.125)
EDGE, MIDDLE, HALF = 0.125, 0.75, 0.5
TAPS = 11
RADIUS = 5

FX, FROW = 5, 8
MX, TX = 6, 6


def messages():
    fine, middle, top = [], [], []
    for dx in (-1, 0, 1):
        sx = {1: (43, 5), 0: (0, 48), -1: (0, 5)}[dx]
        tx = {1: 0, 0: 5, -1: 53}[dx]
        for dy in (-1, 0, 1):
            if dx == 0 and dy == 0:
                continue
            sy = {1: (3, 5), 0: (0, 8), -1: (0, 5)}[dy]
            ty = {1: 3, 0: 8, -1: 16}[dy]
            fine.append((dx, dy, sx, sy, tx, ty))
    for dx in (0, -1, 1):
        sx = {1: (24, 6), 0: (6, 24), -1: (6, 6)}[dx]
        tx = {1: 0, 0: 6, -1: 30}[dx]
        for dy in (-2, -1, 0, 1, 2):
            if dx == 0 and dy == 0:
                continue
            sy = {2: (10, 2), 1: (8, 4), 0: (8, 4), -1: (8, 4), -2: (8, 2)}[dy]
            ty = {2: 2, 1: 4, 0: 8, -1: 12, -2: 16}[dy]
            middle.append((dx, dy, sx, sy, tx, ty))
    for dx in (0, -1, 1):
        sx = {1: (12, 6), 0: (6, 12), -1: (6, 7)}[dx]
        tx = {1: 0, 0: 6, -1: 18}[dx]
        for dy in (-4, -3, -2, -1, 0, 1, 2, 3):
            if dx == 0 and dy == 0:
                continue
            top.append((dx, dy, sx, (8, 2), tx, 8 - 2 * dy))
    return fine, middle, top


FINE, MIDDLE_MSG, TOP = messages()
COUNT = len(FINE) + len(MIDDLE_MSG) + len(TOP)
REACH = 4


def split(value):
    high = value.astype(BF)
    return high, (value - high.astype(F32)).astype(BF)


def dot(a, b):
    return jnp.dot(a, b, preferred_element_type=F32)


def exact_dot(value, weights):
    high, low = split(value)
    return dot(high, weights) + dot(low, weights)


def base_rows(kernel_ref, padded, rows, z):
    per = 128 // z
    padded[...] = jnp.zeros_like(padded)
    padded[0:TAPS, 0:TAPS, 0:TAPS] = kernel_ref[...]
    tap = lax.broadcasted_iota(jnp.int32, (128, per * 128), 0)
    lane = lax.broadcasted_iota(jnp.int32, (128, per * 128), 1)
    place = (lane // 128) * z + RADIUS - tap
    spread = ((lane - place) % 128 == 0) & (tap < TAPS)
    spread = spread.astype(F32).astype(BF)
    table = exact_dot(padded[...].reshape(256, 128), spread).reshape(16, 16, per * 128)
    for n in range(rows.shape[0]):
        total = None
        for q in range(per):
            piece = table[n * per + q, :, q * 128 : (q + 1) * 128]
            total = piece if total is None else total + piece
        rows[n] = total


def toeplitz(rows, high_ref, low_ref, z, depth):
    groups = rows.shape[0] // 2
    lane = lax.broadcasted_iota(jnp.int32, (16, 128), 1) % z
    early, late = lane < z - 8, lane >= 8

    def group(i, _):
        for half in range(2):
            for b in range(TAPS):
                row = jnp.broadcast_to(rows[2 * i + half, b : b + 1, :], (16, 128))
                tile = pltpu.roll(row, 0, 1, stride=1, stride_axis=0)
                for t in range(z // 16):
                    part = pltpu.roll(tile, 16 * t, 1) if t else tile
                    if t == 0:
                        part = jnp.where(early, part, 0.0)
                    if t == z // 16 - 1:
                        part = jnp.where(late, part, 0.0)
                    high, low = split(part)
                    start = pl.multiple_of(i * depth + b * z + 16 * t, 16)
                    high_ref[pl.ds(start, 16), half * 128 : half * 128 + 128] = high
                    low_ref[pl.ds(start, 16), half * 128 : half * 128 + 128] = low
        if depth > TAPS * z:
            start = pl.multiple_of(i * depth + TAPS * z, 16)
            for ref in (high_ref, low_ref):
                ref[pl.ds(start, depth - TAPS * z), :] = jnp.zeros((depth - TAPS * z, 256), BF)
        return 0

    lax.fori_loop(0, groups, group, 0)


def gather_taps(window, high_ref, low_ref, first_row, z):
    per = 128 // z

    def pair(p, _):
        for lane_block in range(high_ref.shape[2] // 128):
            pieces = []
            for q in range(per):
                row = first_row + lane_block * per + q
                pieces.append(window[pl.ds(2 * p, 2), row : row + 8, :])
            value = pieces[0] if per == 1 else jnp.concatenate(pieces, axis=-1)
            high, low = split(value.reshape(16, 128))
            at = slice(lane_block * 128, lane_block * 128 + 128)
            high_ref[p, :, at] = high
            low_ref[p, :, at] = low
        return 0

    lax.fori_loop(0, high_ref.shape[0], pair, 0)


def products(ah, al, wh, wl):
    return dot(ah, wh) + dot(al, wh) + dot(ah, wl)


def small_convolution(high_a, low_a, high_w, low_w, pairs, step, groups, depth, z, planes):
    total = None
    for i in range(groups):
        ah = high_a[i * step : i * step + pairs].reshape(pairs * 16, depth)
        al = low_a[i * step : i * step + pairs].reshape(pairs * 16, depth)
        at = slice(i * depth, (i + 1) * depth)
        part = products(ah, al, high_w[at], low_w[at])
        total = part if total is None else total + part
    total = total.reshape(pairs * 2, 8, 256)
    result = None
    for j in range(256 // z):
        piece = total[j : j + planes, :, j * z : (j + 1) * z]
        result = piece if result is None else result + piece
    return result


def fine_step(i, high_a, low_a, high_w, low_w, total):
    def rows(ref):
        first = ref[pl.ds(2 * i, 25)].reshape(400, 1408)
        second = ref[pl.ds(2 * i + 1, 25)].reshape(400, 1408)
        return jnp.concatenate([first, second], axis=-1)

    at = pl.ds(pl.multiple_of(i * 2816, 2816), 2816)
    total[...] += products(rows(high_a), rows(low_a), high_w[at], low_w[at])


def restrict_matrix(z):
    source = lax.broadcasted_iota(jnp.int32, (z, z // 2), 0)
    target = lax.broadcasted_iota(jnp.int32, (z, z // 2), 1)
    away = jnp.abs(source - 2 * target)
    weight = jnp.where(away == 0, 0.75, jnp.where(away == 1, 0.5, jnp.where(away == 2, 0.125, 0.0)))
    return weight.astype(F32).astype(BF)


def prolong_matrix(z):
    source = lax.broadcasted_iota(jnp.int32, (z, 2 * z), 0)
    target = lax.broadcasted_iota(jnp.int32, (z, 2 * z), 1)
    away = jnp.abs(target - 2 * source)
    weight = jnp.where(away == 0, 0.75, jnp.where(away == 1, 0.5, jnp.where(away == 2, 0.125, 0.0)))
    return weight.astype(F32).astype(BF)


def restrict(window, along_x, first_plane, first_row, planes, z):
    for i in range(planes):
        total = None
        for a, weight in enumerate(SPLINE):
            piece = weight * window[first_plane + 2 * i + a - 2]
            total = piece if total is None else total + piece
        along_x[i, 0:24, :] = total
    rows = None
    for b, weight in enumerate(SPLINE):
        piece = weight * along_x[:, pl.ds(first_row + b - 2, 8, stride=2), :]
        rows = piece if rows is None else rows + piece
    result = exact_dot(rows.reshape(planes * 8, z), restrict_matrix(z))
    return result.reshape(planes, 8, z // 2)


def inside(planes, first_x, count_x, first_y, count_y, z):
    x = first_x + lax.broadcasted_iota(jnp.int32, (planes, 8, z), 0)
    y = first_y + lax.broadcasted_iota(jnp.int32, (planes, 8, z), 1)
    return (x >= 0) & (x < count_x) & (y >= 0) & (y < count_y)


def whole(
    nx, ny,
    charge, kernel_fine, kernel_mid, kernel_top, out,
    fine, along_fine, middle, along_middle, top, padded, rows_f, rows_m, rows_t,
    wfh, wfl, wmh, wml, wth, wtl, afh, afl, amh, aml, ath, atl,
    total, pot_z, pot_y, top_z, top_y, send_sems, recv_sems,
):
    gx, gy = lax.axis_index("gx"), lax.axis_index("gy")

    def exists(dx, dy):
        return (gx + dx >= 0) & (gx + dx < nx) & (gy + dy >= 0) & (gy + dy < ny)

    def transfer(number, message, source, target):
        dx, dy, (px, lx), (py, ly), tx, ty = message
        return pltpu.make_async_remote_copy(
            src_ref=source.at[pl.ds(px, lx), pl.ds(py, ly)],
            dst_ref=target.at[pl.ds(tx, lx), pl.ds(ty, ly)],
            send_sem=send_sems.at[number],
            recv_sem=recv_sems.at[number],
            device_id={"gx": gx + dx, "gy": gy + dy},
            device_id_type=pl.DeviceIdType.MESH,
        )

    def start(first, group, source, target):
        for k, message in enumerate(group):
            @pl.when(exists(message[0], message[1]))
            def _(k=k, message=message):
                transfer(first + k, message, source, target).start()

    def arrive(first, group, source, target):
        for k, message in enumerate(group):
            @pl.when(exists(-message[0], -message[1]))
            def _(k=k, message=message):
                transfer(first + k, message, source, target).wait_recv()

    def sent(first, group, source, target):
        for k, message in enumerate(group):
            @pl.when(exists(message[0], message[1]))
            def _(k=k, message=message):
                transfer(first + k, message, source, target).wait_send()

    n_fine, n_middle = len(FINE), len(FINE) + len(MIDDLE_MSG)

    fine[...] = jnp.zeros_like(fine)
    fine[FX : FX + 48, FROW : FROW + 8, :] = charge[...]
    middle[...] = jnp.zeros_like(middle)
    top[...] = jnp.zeros_like(top)
    along_fine[...] = jnp.zeros_like(along_fine)
    along_middle[...] = jnp.zeros_like(along_middle)

    barrier = pltpu.get_barrier_semaphore()
    for dx in (-1, 0, 1):
        for dy in range(-REACH, REACH + 1):
            if dx == 0 and dy == 0:
                continue
            @pl.when(exists(dx, dy))
            def _(dx=dx, dy=dy):
                pl.semaphore_signal(
                    barrier, inc=1, device_id={"gx": gx + dx, "gy": gy + dy},
                    device_id_type=pl.DeviceIdType.MESH,
                )

    base_rows(kernel_mid, padded, rows_m, 64)
    toeplitz(rows_m, wmh, wml, 64, 768)
    base_rows(kernel_top, padded, rows_t, 32)
    toeplitz(rows_t, wth, wtl, 32, 384)
    base_rows(kernel_fine, padded, rows_f, 128)

    across = 1 + (gx > 0).astype(jnp.int32) + (gx < nx - 1).astype(jnp.int32)
    along = 1 + jnp.minimum(gy, REACH) + jnp.minimum(ny - 1 - gy, REACH)
    pl.semaphore_wait(barrier, across * along - 1)

    start(0, FINE, charge, fine)
    toeplitz(rows_f, wfh, wfl, 128, 1408)
    arrive(0, FINE, charge, fine)

    middle_block = restrict(fine, along_fine, FX, FROW, 24, 128)
    middle[MX : MX + 24, 8:12, :] = middle_block[:, 0:4, :]
    start(n_fine, MIDDLE_MSG, middle, middle)

    gather_taps(fine, afh, afl, 3, 128)
    total[...] = jnp.zeros_like(total)
    fine_step(0, afh, afl, wfh, wfl, total)

    arrive(n_fine, MIDDLE_MSG, middle, middle)
    top_block = restrict(middle, along_middle, MX, 8, 12, 64)
    top[TX : TX + 12, 8:10, :] = top_block[:, 0:2, :]
    start(n_middle, TOP, top, top)

    def step(i, _):
        fine_step(i, afh, afl, wfh, wfl, total)
        return 0

    lax.fori_loop(1, 3, step, 0)
    gather_taps(middle, amh, aml, 2, 64)

    arrive(n_middle, TOP, top, top)
    gather_taps(top, ath, atl, 2, 32)
    top_pot = small_convolution(ath, atl, wth, wtl, 11, 4, 2, 384, 32, 15)
    top_pot = jnp.where(inside(15, gx * 12 - 1, nx * 12, gy * 2 - 1, ny * 2, 32), top_pot, 0.0)
    top_z[...] = exact_dot(top_pot.reshape(120, 32), prolong_matrix(32)).reshape(15, 8, 64)
    e0, e1, e2 = top_z[:, 0:3, :], top_z[:, 1:4, :], top_z[:, 2:5, :]
    top_y[...] = jnp.zeros_like(top_y)
    top_y[:, pl.ds(0, 3, stride=2), :] = HALF * e0 + HALF * e1
    top_y[:, pl.ds(1, 3, stride=2), :] = EDGE * e0 + MIDDLE * e1 + EDGE * e2

    mid_pot = small_convolution(amh, aml, wmh, wml, 15, 2, 3, 768, 64, 26)
    pieces = []
    for k in range(13):
        f0, f1, f2 = top_y[k], top_y[k + 1], top_y[k + 2]
        pieces.append((HALF * f0 + HALF * f1)[None])
        pieces.append((EDGE * f0 + MIDDLE * f1 + EDGE * f2)[None])
    mid_pot = mid_pot + jnp.concatenate(pieces, axis=0)
    mid_pot = jnp.where(inside(26, gx * 24 - 1, nx * 24, gy * 4 - 1, ny * 4, 64), mid_pot, 0.0)
    pot_z[...] = exact_dot(mid_pot.reshape(208, 64), prolong_matrix(64)).reshape(26, 8, 128)
    e0, e1, e2 = pot_z[:, 0:4, :], pot_z[:, 1:5, :], pot_z[:, 2:6, :]
    pot_y[:, pl.ds(0, 4, stride=2), :] = EDGE * e0 + MIDDLE * e1 + EDGE * e2
    pot_y[:, pl.ds(1, 4, stride=2), :] = HALF * e1 + HALF * e2

    for m in range(24):
        f0, f1, f2 = pot_y[m], pot_y[m + 1], pot_y[m + 2]
        for odd in range(2):
            x = 2 * m + odd
            near = total[8 * x : 8 * x + 8, 0:128]
            far = total[8 * x + 8 : 8 * x + 16, 128:256]
            fill = HALF * f1 + HALF * f2 if odd else EDGE * f0 + MIDDLE * f1 + EDGE * f2
            out[x] = near + far + fill

    sent(0, FINE, charge, fine)
    sent(n_fine, MIDDLE_MSG, middle, middle)
    sent(n_middle, TOP, top, top)


def solution(mesh):
    nx, ny = mesh.shape["gx"], mesh.shape["gy"]
    vmem = pltpu.VMEM
    scratch = [
        vmem((60, 24, 128), F32), vmem((24, 32, 128), F32), vmem((40, 24, 64), F32),
        vmem((12, 32, 64), F32), vmem((32, 24, 32), F32), vmem((16, 16, 128), F32),
        vmem((12, 16, 128), F32), vmem((6, 16, 128), F32), vmem((4, 16, 128), F32),
        vmem((8448, 256), BF), vmem((8448, 256), BF), vmem((2304, 256), BF), vmem((2304, 256), BF),
        vmem((768, 256), BF), vmem((768, 256), BF),
        vmem((30, 16, 1408), BF), vmem((30, 16, 1408), BF), vmem((19, 16, 768), BF),
        vmem((19, 16, 768), BF), vmem((15, 16, 384), BF), vmem((15, 16, 384), BF),
        vmem((400, 256), F32), vmem((26, 8, 128), F32), vmem((26, 8, 128), F32),
        vmem((15, 8, 64), F32), vmem((15, 8, 64), F32),
        pltpu.SemaphoreType.DMA((COUNT,)), pltpu.SemaphoreType.DMA((COUNT,)),
    ]

    def shards(charge, kernel_fine, kernel_mid, kernel_top):
        return pl.pallas_call(
            functools.partial(whole, nx, ny),
            out_shape=jax.ShapeDtypeStruct(charge.shape, F32),
            in_specs=[pl.BlockSpec(memory_space=pltpu.VMEM)] * 4,
            out_specs=pl.BlockSpec(memory_space=pltpu.VMEM),
            scratch_shapes=scratch,
            compiler_params=pltpu.CompilerParams(
                collective_id=0, has_side_effects=True, vmem_limit_bytes=60 << 20
            ),
            name="multilevel",
        )(charge, kernel_fine, kernel_mid, kernel_top)

    return jax.shard_map(
        shards, mesh=mesh, in_specs=(P("gx", "gy", None), P(), P(), P()),
        out_specs=P("gx", "gy", None), check_vma=False,
    )
```

time: 322 us -> 33 us (0.10)
  matrix products: 118 us -> 0 us
  local copies, waits for them, and re-layouts: 93.2 us -> 1.62 us
  starting transfers between devices: 73.5 us -> 0 us
  Pallas kernels: 0 us -> 31.3 us
  other arithmetic: 23.2 us -> 0 us
  waiting for transfers between devices: 9.3 us -> 0 us
    dot_general x36 -> x0, matrix products: 118 us -> none  [the longest x33 101 us: add_plane(): jnp.dot(plane.reshape(-1, window), weights, precision=HIGHEST, preferred_...]
    ppermute x22 -> x0, starting transfers between devices: 73.5 us -> none  [the longest x12 42.5 us: from_behind(): lax.ppermute(value, axis, [(source, source + steps) for source in range(l...]
    dynamic_slice x44 -> x0, local copies, waits for them, and re-layouts: 58.8 us -> none  [add_plane(): weights = lax.dynamic_index_in_dim(matrices, plane_index, 0, keepdims=False)]
    pallas_call x0 -> x1, Pallas kernels: none -> 31.3 us  [shards(): pl.pallas_call(functools.partial(whole, nx, ny), out_shape=jax.ShapeDtype...]
    add x41 -> x0, other arithmetic: 22.1 us -> none  [the longest x33 21.8 us: add_plane(): total = total + product[:, offset:offset + width_y, :, offset, :]]
    reshape x1 -> x0, local copies, waits for them, and re-layouts: 13.6 us -> none  [convolve(): matrices = band_matrices(kernel, block_len).transpose(0, 2, 1, 3).reshape...]
    ppermute x22 -> x0, waiting for transfers between devices: 9.3 us -> none  [the longest x5 5.84 us: with_halo(): lax.ppermute(head, axis, [((i + 1) % count, i) for i in range(ends)])]
    transpose x2 -> x0, local copies, waits for them, and re-layouts: 7.78 us -> none  [convolve(): matrices = band_matrices(kernel, block_len).transpose(0, 2, 1, 3).reshape...]
  transfers between devices with their start and end apart: 22 -> 0, of which waited for: 5 -> 0; matrix products, arithmetic and copies ran while one was open for 62% -> 0% of each run, Pallas kernels for 0% -> 0%
where the time goes in v1:
time: 33 us; the launch traced here: 32.9 us
  Pallas kernels  31.3 us (95%)
  local copies, waits for them, and re-layouts  1.62 us (5%)
    pallas_call x1, Pallas kernels, shards(): pl.pallas_call(functools.partial(whole, nx, ny), out_shape=jax.ShapeDtype...  31.3 us
    unnamed x1, local copies, waits for them, and re-layouts  1.62 us

profile of v1, /device:TPU:26, one launch (start us, length us, event | category | flops | bytes accessed | tf_op | source)
XLA Modules:
  0.0 32.9 jit_solution(6983918225911228726)
XLA Ops:
  0.0 31.3 %multilevel.1 = f32[48,8,128]{2,1,0:T(8,128)} custom-call(f32[48,8,128]{2,1,0:T(8,128)} %charge.1, f32[11,11,11]{2,1,0:T(8,128)} %kernel_fine.1, f32[11,11,11]{2,1,0:T(8,128)} %kernel_mid.1, f32[11,11,11]{2,1,0:T(8,128)} %kernel_top.1), custom_call_target="tpu_custom_call" | custom-call | tf_op jit(solution)/shard_map/multilevel/pallas_call | solution.py:353
  31.3 1.6 %copy.6 = f32[48,8,128]{2,1,0:T(8,128)} copy(f32[48,8,128]{2,1,0:T(8,128)} %multilevel.1) | data formatting | bytes 393216

commit v2 on v1

--- a/solution.py
+++ b/solution.py
@@ -14,43 +14,38 @@
 TAPS = 11
 RADIUS = 5
 
-FX, FROW = 5, 8
+FX, FROW = 6, 8
 MX, TX = 6, 6
+REACH = 4
 
 
 def messages():
     fine, middle, top = [], [], []
     for dx in (-1, 0, 1):
-        sx = {1: (43, 5), 0: (0, 48), -1: (0, 5)}[dx]
-        tx = {1: 0, 0: 5, -1: 53}[dx]
+        sx = {1: (42, 6), 0: (0, 48), -1: (0, 5)}[dx]
+        tx = {1: 0, 0: 6, -1: 54}[dx]
         for dy in (-1, 0, 1):
-            if dx == 0 and dy == 0:
-                continue
-            sy = {1: (3, 5), 0: (0, 8), -1: (0, 5)}[dy]
-            ty = {1: 3, 0: 8, -1: 16}[dy]
+            sy = {1: (2, 6), 0: (0, 8), -1: (0, 5)}[dy]
+            ty = {1: 2, 0: 8, -1: 16}[dy]
             fine.append((dx, dy, sx, sy, tx, ty))
-    for dx in (0, -1, 1):
         sx = {1: (24, 6), 0: (6, 24), -1: (6, 6)}[dx]
         tx = {1: 0, 0: 6, -1: 30}[dx]
-        for dy in (-2, -1, 0, 1, 2):
-            if dx == 0 and dy == 0:
-                continue
-            sy = {2: (10, 2), 1: (8, 4), 0: (8, 4), -1: (8, 4), -2: (8, 2)}[dy]
+        for dy in range(-2, 3):
+            sy = {2: (10, 2), -2: (8, 2)}.get(dy, (8, 4))
             ty = {2: 2, 1: 4, 0: 8, -1: 12, -2: 16}[dy]
             middle.append((dx, dy, sx, sy, tx, ty))
-    for dx in (0, -1, 1):
         sx = {1: (12, 6), 0: (6, 12), -1: (6, 7)}[dx]
         tx = {1: 0, 0: 6, -1: 18}[dx]
-        for dy in (-4, -3, -2, -1, 0, 1, 2, 3):
-            if dx == 0 and dy == 0:
-                continue
+        for dy in range(-4, 4):
             top.append((dx, dy, sx, (8, 2), tx, 8 - 2 * dy))
-    return fine, middle, top
+    return [[m for m in group if m[:2] != (0, 0)] for group in (fine, middle, top)]
 
 
 FINE, MIDDLE_MSG, TOP = messages()
-COUNT = len(FINE) + len(MIDDLE_MSG) + len(TOP)
-REACH = 4
+EVERY = FINE + MIDDLE_MSG + TOP
+COUNT = len(EVERY)
+N_FINE = len(FINE)
+N_MIDDLE = N_FINE + len(MIDDLE_MSG)
 
 
 def split(value):
@@ -85,26 +80,42 @@
         rows[n] = total
 
 
-def toeplitz(rows, high_ref, low_ref, z, depth):
-    groups = rows.shape[0] // 2
-    lane = lax.broadcasted_iota(jnp.int32, (16, 128), 1) % z
-    early, late = lane < z - 8, lane >= 8
+def shift_matrix(z, first, tiles):
+    source = lax.broadcasted_iota(jnp.int32, (128, tiles * 128), 0)
+    target = lax.broadcasted_iota(jnp.int32, (128, tiles * 128), 1)
+    ahead = 16 * (target // 128 + first)
+    cell = target % z
+    keep = ((source + ahead - target) % 128 == 0) & (cell >= ahead - RADIUS) & (cell <= ahead + 20)
+    return keep.astype(F32).astype(BF)
+
+
+def toeplitz(rows, high_ref, low_ref, z, depth, rolled):
+    groups, tiles = rows.shape[0] // 2, z // 16
+    shifts = shift_matrix(z, rolled, tiles - rolled)
+    early = lax.broadcasted_iota(jnp.int32, (16, 128), 1) % z < z - 8
 
     def group(i, _):
         for half in range(2):
+            at = slice(half * 128, half * 128 + 128)
+
+            def place(ref, b, t, tile):
+                ref[pl.ds(pl.multiple_of(i * depth + b * z + 16 * t, 16), 16), at] = tile
+
+            firsts = []
             for b in range(TAPS):
                 row = jnp.broadcast_to(rows[2 * i + half, b : b + 1, :], (16, 128))
-                tile = pltpu.roll(row, 0, 1, stride=1, stride_axis=0)
-                for t in range(z // 16):
-                    part = pltpu.roll(tile, 16 * t, 1) if t else tile
-                    if t == 0:
-                        part = jnp.where(early, part, 0.0)
-                    if t == z // 16 - 1:
-                        part = jnp.where(late, part, 0.0)
-                    high, low = split(part)
-                    start = pl.multiple_of(i * depth + b * z + 16 * t, 16)
-                    high_ref[pl.ds(start, 16), half * 128 : half * 128 + 128] = high
-                    low_ref[pl.ds(start, 16), half * 128 : half * 128 + 128] = low
+                firsts.append(pltpu.roll(row, 0, 1, stride=1, stride_axis=0))
+            for part, ref in zip(split(jnp.concatenate(firsts, axis=0)), (high_ref, low_ref)):
+                moved = dot(part, shifts).astype(BF)
+                for b in range(TAPS):
+                    for t in range(rolled, tiles):
+                        lanes = slice(128 * (t - rolled), 128 * (t - rolled) + 128)
+                        place(ref, b, t, moved[16 * b : 16 * b + 16, lanes])
+            for b in range(TAPS):
+                for t in range(rolled):
+                    tile = pltpu.roll(firsts[b], 16 * t, 1) if t else jnp.where(early, firsts[b], 0.0)
+                    for part, ref in zip(split(tile), (high_ref, low_ref)):
+                        place(ref, b, t, part)
         if depth > TAPS * z:
             start = pl.multiple_of(i * depth + TAPS * z, 16)
             for ref in (high_ref, low_ref):
@@ -114,7 +125,7 @@
     lax.fori_loop(0, groups, group, 0)
 
 
-def gather_taps(window, high_ref, low_ref, first_row, z):
+def gather_taps(window, high_ref, low_ref, first_plane, first_row, z):
     per = 128 // z
 
     def pair(p, _):
@@ -122,7 +133,7 @@
             pieces = []
             for q in range(per):
                 row = first_row + lane_block * per + q
-                pieces.append(window[pl.ds(2 * p, 2), row : row + 8, :])
+                pieces.append(window[pl.ds(first_plane + 2 * p, 2), row : row + 8, :])
             value = pieces[0] if per == 1 else jnp.concatenate(pieces, axis=-1)
             high, low = split(value.reshape(16, 128))
             at = slice(lane_block * 128, lane_block * 128 + 128)
@@ -159,7 +170,7 @@
         second = ref[pl.ds(2 * i + 1, 25)].reshape(400, 1408)
         return jnp.concatenate([first, second], axis=-1)
 
-    at = pl.ds(pl.multiple_of(i * 2816, 2816), 2816)
+    at = pl.ds(i * 2816, 2816)
     total[...] += products(rows(high_a), rows(low_a), high_w[at], low_w[at])
 
 
@@ -179,16 +190,19 @@
     return weight.astype(F32).astype(BF)
 
 
-def restrict(window, along_x, first_plane, first_row, planes, z):
+def restrict(block, along_x, first_plane, first_row, at, z):
+    planes = along_x.shape[0]
     for i in range(planes):
         total = None
         for a, weight in enumerate(SPLINE):
-            piece = weight * window[first_plane + 2 * i + a - 2]
-            total = piece if total is None else total + piece
-        along_x[i, 0:24, :] = total
+            source = first_plane + 2 * i + a
+            if 0 <= source < block.shape[0]:
+                piece = weight * block[source]
+                total = piece if total is None else total + piece
+        along_x[i, at : at + block.shape[1], :] = total
     rows = None
     for b, weight in enumerate(SPLINE):
-        piece = weight * along_x[:, pl.ds(first_row + b - 2, 8, stride=2), :]
+        piece = weight * along_x[:, pl.ds(first_row + b, 8, stride=2), :]
         rows = piece if rows is None else rows + piece
     result = exact_dot(rows.reshape(planes * 8, z), restrict_matrix(z))
     return result.reshape(planes, 8, z // 2)
@@ -202,53 +216,62 @@
 
 def whole(
     nx, ny,
-    charge, kernel_fine, kernel_mid, kernel_top, out,
-    fine, along_fine, middle, along_middle, top, padded, rows_f, rows_m, rows_t,
+    charge_hbm, kernel_fine_hbm, kernel_mid_hbm, kernel_top_hbm, out,
+    charge, kernel_fine, kernel_mid, kernel_top,
+    fine, along_fine, middle, along_middle, top,
+    padded, rows_f, rows_m, rows_t,
     wfh, wfl, wmh, wml, wth, wtl, afh, afl, amh, aml, ath, atl,
-    total, pot_z, pot_y, top_z, top_y, send_sems, recv_sems,
+    total, pot_z, pot_y, top_z, top_y, load_sems, send_sems, recv_sems,
 ):
     gx, gy = lax.axis_index("gx"), lax.axis_index("gy")
 
+    loads = [
+        pltpu.make_async_copy(source, target, load_sems.at[n])
+        for n, (source, target) in enumerate((
+            (charge_hbm, charge), (kernel_mid_hbm, kernel_mid),
+            (kernel_top_hbm, kernel_top), (kernel_fine_hbm, kernel_fine),
+        ))
+    ]
+    for load in loads:
+        load.start()
+
     def exists(dx, dy):
         return (gx + dx >= 0) & (gx + dx < nx) & (gy + dy >= 0) & (gy + dy < ny)
 
-    def transfer(number, message, source, target):
-        dx, dy, (px, lx), (py, ly), tx, ty = message
+    def transfer(number):
+        dx, dy, (px, lx), (py, ly), tx, ty = EVERY[number]
+        if number < N_FINE:
+            source, target = charge, fine.at[pl.ds(tx, lx), pl.ds(ty, ly)]
+        else:
+            source = middle if number < N_MIDDLE else top
+            target = source.at[pl.ds(tx, lx), pl.ds(ty, ly)]
         return pltpu.make_async_remote_copy(
-            src_ref=source.at[pl.ds(px, lx), pl.ds(py, ly)],
-            dst_ref=target.at[pl.ds(tx, lx), pl.ds(ty, ly)],
-            send_sem=send_sems.at[number],
-            recv_sem=recv_sems.at[number],
+            src_ref=source.at[pl.ds(px, lx), pl.ds(py, ly)], dst_ref=target,
+            send_sem=send_sems.at[number], recv_sem=recv_sems.at[number],
             device_id={"gx": gx + dx, "gy": gy + dy},
             device_id_type=pl.DeviceIdType.MESH,
         )
 
-    def start(first, group, source, target):
-        for k, message in enumerate(group):
-            @pl.when(exists(message[0], message[1]))
-            def _(k=k, message=message):
-                transfer(first + k, message, source, target).start()
-
-    def arrive(first, group, source, target):
-        for k, message in enumerate(group):
-            @pl.when(exists(-message[0], -message[1]))
-            def _(k=k, message=message):
-                transfer(first + k, message, source, target).wait_recv()
-
-    def sent(first, group, source, target):
-        for k, message in enumerate(group):
-            @pl.when(exists(message[0], message[1]))
-            def _(k=k, message=message):
-                transfer(first + k, message, source, target).wait_send()
-
-    n_fine, n_middle = len(FINE), len(FINE) + len(MIDDLE_MSG)
-
-    fine[...] = jnp.zeros_like(fine)
-    fine[FX : FX + 48, FROW : FROW + 8, :] = charge[...]
-    middle[...] = jnp.zeros_like(middle)
-    top[...] = jnp.zeros_like(top)
-    along_fine[...] = jnp.zeros_like(along_fine)
-    along_middle[...] = jnp.zeros_like(along_middle)
+    def start(numbers):
+        for number in numbers:
+            @pl.when(exists(EVERY[number][0], EVERY[number][1]))
+            def _(number=number):
+                transfer(number).start()
+
+    def arrive(numbers):
+        for number in numbers:
+            @pl.when(exists(-EVERY[number][0], -EVERY[number][1]))
+            def _(number=number):
+                transfer(number).wait_recv()
+
+    def sent(numbers):
+        for number in numbers:
+            @pl.when(exists(EVERY[number][0], EVERY[number][1]))
+            def _(number=number):
+                transfer(number).wait_send()
+
+    for ref in (fine, middle, top):
+        ref[...] = jnp.zeros_like(ref)
 
     barrier = pltpu.get_barrier_semaphore()
     for dx in (-1, 0, 1):
@@ -262,42 +285,42 @@
                     device_id_type=pl.DeviceIdType.MESH,
                 )
 
+    for ref in (along_fine, along_middle):
+        ref[...] = jnp.zeros_like(ref)
+    for load in loads:
+        load.wait()
+
+    fine[FX : FX + 48, FROW : FROW + 8, :] = charge[...]
     base_rows(kernel_mid, padded, rows_m, 64)
-    toeplitz(rows_m, wmh, wml, 64, 768)
+    toeplitz(rows_m, wmh, wml, 64, 768, 2)
     base_rows(kernel_top, padded, rows_t, 32)
-    toeplitz(rows_t, wth, wtl, 32, 384)
+    toeplitz(rows_t, wth, wtl, 32, 384, 1)
     base_rows(kernel_fine, padded, rows_f, 128)
 
     across = 1 + (gx > 0).astype(jnp.int32) + (gx < nx - 1).astype(jnp.int32)
     along = 1 + jnp.minimum(gy, REACH) + jnp.minimum(ny - 1 - gy, REACH)
     pl.semaphore_wait(barrier, across * along - 1)
 
-    start(0, FINE, charge, fine)
-    toeplitz(rows_f, wfh, wfl, 128, 1408)
-    arrive(0, FINE, charge, fine)
-
-    middle_block = restrict(fine, along_fine, FX, FROW, 24, 128)
-    middle[MX : MX + 24, 8:12, :] = middle_block[:, 0:4, :]
-    start(n_fine, MIDDLE_MSG, middle, middle)
-
-    gather_taps(fine, afh, afl, 3, 128)
+    start(range(N_FINE))
+    toeplitz(rows_f, wfh, wfl, 128, 1408, 5)
+    arrive(range(N_FINE))
+
+    near = restrict(fine, along_fine, 0, 2, 0, 128)
+    near = jnp.where(inside(27, gx * 24 - 2, nx * 24, gy * 4 - 2, ny * 4, 64), near, 0.0)
+    middle[MX : MX + 24, 8:12, :] = near[2:26, 2:6, :]
+    top[TX : TX + 12, 8:10, :] = restrict(near, along_middle, 0, 8, 8, 64)[:, 0:2, :]
+    start(range(N_FINE, COUNT))
+
+    gather_taps(fine, afh, afl, 1, 3, 128)
     total[...] = jnp.zeros_like(total)
-    fine_step(0, afh, afl, wfh, wfl, total)
-
-    arrive(n_fine, MIDDLE_MSG, middle, middle)
-    top_block = restrict(middle, along_middle, MX, 8, 12, 64)
-    top[TX : TX + 12, 8:10, :] = top_block[:, 0:2, :]
-    start(n_middle, TOP, top, top)
-
-    def step(i, _):
+
+    for i in range(3):
         fine_step(i, afh, afl, wfh, wfl, total)
-        return 0
-
-    lax.fori_loop(1, 3, step, 0)
-    gather_taps(middle, amh, aml, 2, 64)
-
-    arrive(n_middle, TOP, top, top)
-    gather_taps(top, ath, atl, 2, 32)
+
+    arrive(range(N_FINE, N_MIDDLE))
+    gather_taps(middle, amh, aml, 0, 2, 64)
+    arrive(range(N_MIDDLE, COUNT))
+    gather_taps(top, ath, atl, 0, 2, 32)
     top_pot = small_convolution(ath, atl, wth, wtl, 11, 4, 2, 384, 32, 15)
     top_pot = jnp.where(inside(15, gx * 12 - 1, nx * 12, gy * 2 - 1, ny * 2, 32), top_pot, 0.0)
     top_z[...] = exact_dot(top_pot.reshape(120, 32), prolong_matrix(32)).reshape(15, 8, 64)
@@ -328,16 +351,16 @@
             fill = HALF * f1 + HALF * f2 if odd else EDGE * f0 + MIDDLE * f1 + EDGE * f2
             out[x] = near + far + fill
 
-    sent(0, FINE, charge, fine)
-    sent(n_fine, MIDDLE_MSG, middle, middle)
-    sent(n_middle, TOP, top, top)
+    sent(range(COUNT))
 
 
 def solution(mesh):
     nx, ny = mesh.shape["gx"], mesh.shape["gy"]
     vmem = pltpu.VMEM
     scratch = [
-        vmem((60, 24, 128), F32), vmem((24, 32, 128), F32), vmem((40, 24, 64), F32),
+        vmem((48, 8, 128), F32), vmem((11, 11, 11), F32), vmem((11, 11, 11), F32),
+        vmem((11, 11, 11), F32),
+        vmem((62, 24, 128), F32), vmem((27, 32, 128), F32), vmem((40, 24, 64), F32),
         vmem((12, 32, 64), F32), vmem((32, 24, 32), F32), vmem((16, 16, 128), F32),
         vmem((12, 16, 128), F32), vmem((6, 16, 128), F32), vmem((4, 16, 128), F32),
         vmem((8448, 256), BF), vmem((8448, 256), BF), vmem((2304, 256), BF), vmem((2304, 256), BF),
@@ -346,6 +369,7 @@
         vmem((19, 16, 768), BF), vmem((15, 16, 384), BF), vmem((15, 16, 384), BF),
         vmem((400, 256), F32), vmem((26, 8, 128), F32), vmem((26, 8, 128), F32),
         vmem((15, 8, 64), F32), vmem((15, 8, 64), F32),
+        pltpu.SemaphoreType.DMA((4,)),
         pltpu.SemaphoreType.DMA((COUNT,)), pltpu.SemaphoreType.DMA((COUNT,)),
     ]
 
@@ -353,7 +377,7 @@
         return pl.pallas_call(
             functools.partial(whole, nx, ny),
             out_shape=jax.ShapeDtypeStruct(charge.shape, F32),
-            in_specs=[pl.BlockSpec(memory_space=pltpu.VMEM)] * 4,
+            in_specs=[pl.BlockSpec(memory_space=pl.ANY)] * 4,
             out_specs=pl.BlockSpec(memory_space=pltpu.VMEM),
             scratch_shapes=scratch,
             compiler_params=pltpu.CompilerParams(

time: 33 us -> 27.8 us (0.84)
  Pallas kernels: 31.3 us -> 26 us
    pallas_call x1, Pallas kernels: 31.3 us -> 26 us  [shards(): pl.pallas_call(functools.partial(whole, nx, ny), out_shape=jax.ShapeDtype...]
where the time goes in v2:
time: 27.8 us; the launch traced here: 27.7 us
  Pallas kernels  26 us (94%)
  local copies, waits for them, and re-layouts  1.62 us (6%)
    pallas_call x1, Pallas kernels, shards(): pl.pallas_call(functools.partial(whole, nx, ny), out_shape=jax.ShapeDtype...  26 us
    unnamed x1, local copies, waits for them, and re-layouts  1.62 us

profile of v2, /device:TPU:26, one launch (start us, length us, event | category | flops | bytes accessed | tf_op | source)
XLA Modules:
  0.0 27.7 jit_solution(12094705358387953689)
XLA Ops:
  0.0 26.0 %multilevel.1 = f32[48,8,128]{2,1,0:T(8,128)} custom-call(f32[48,8,128]{2,1,0:T(8,128)} %charge_hbm.1, f32[11,11,11]{2,1,0:T(8,128)} %kernel_fine_hbm.1, f32[11,11,11]{2,1,0:T(8,128)} %kernel_mid_hbm.1, f32[11,11,11]{2,1,0:T(8,128)} %kernel_top_hbm.1), custom_call_target="tpu_custom_call" | custom-call | tf_op jit(solution)/shard_map/multilevel/pallas_call | solution.py:377
  26.0 1.6 %copy.6 = f32[48,8,128]{2,1,0:T(8,128)} copy(f32[48,8,128]{2,1,0:T(8,128)} %multilevel.1) | data formatting | bytes 393216

commit v3 on v2

--- a/solution.py
+++ b/solution.py
@@ -94,12 +94,12 @@
     shifts = shift_matrix(z, rolled, tiles - rolled)
     early = lax.broadcasted_iota(jnp.int32, (16, 128), 1) % z < z - 8
 
-    def group(i, _):
+    def group(i):
         for half in range(2):
             at = slice(half * 128, half * 128 + 128)
 
             def place(ref, b, t, tile):
-                ref[pl.ds(pl.multiple_of(i * depth + b * z + 16 * t, 16), 16), at] = tile
+                ref[pl.ds(i * depth + b * z + 16 * t, 16), at] = tile
 
             firsts = []
             for b in range(TAPS):
@@ -117,18 +117,18 @@
                     for part, ref in zip(split(tile), (high_ref, low_ref)):
                         place(ref, b, t, part)
         if depth > TAPS * z:
-            start = pl.multiple_of(i * depth + TAPS * z, 16)
+            start = i * depth + TAPS * z
             for ref in (high_ref, low_ref):
                 ref[pl.ds(start, depth - TAPS * z), :] = jnp.zeros((depth - TAPS * z, 256), BF)
-        return 0
-
-    lax.fori_loop(0, groups, group, 0)
+
+    for i in range(groups):
+        group(i)
 
 
 def gather_taps(window, high_ref, low_ref, first_plane, first_row, z):
     per = 128 // z
 
-    def pair(p, _):
+    def pair(p):
         for lane_block in range(high_ref.shape[2] // 128):
             pieces = []
             for q in range(per):
@@ -139,9 +139,9 @@
             at = slice(lane_block * 128, lane_block * 128 + 128)
             high_ref[p, :, at] = high
             low_ref[p, :, at] = low
-        return 0
-
-    lax.fori_loop(0, high_ref.shape[0], pair, 0)
+
+    for p in range(high_ref.shape[0]):
+        pair(p)
 
 
 def products(ah, al, wh, wl):

time: 27.8 us -> 24.1 us (0.87)
  Pallas kernels: 26 us -> 22.1 us
    pallas_call x1, Pallas kernels: 26 us -> 22.1 us  [shards(): pl.pallas_call(functools.partial(whole, nx, ny), out_shape=jax.ShapeDtype...]
where the time goes in v3:
time: 24.1 us; the launch traced here: 23.7 us
  Pallas kernels  22.1 us (92%)
  local copies, waits for them, and re-layouts  1.62 us (7%)
    pallas_call x1, Pallas kernels, shards(): pl.pallas_call(functools.partial(whole, nx, ny), out_shape=jax.ShapeDtype...  22.1 us
    unnamed x1, local copies, waits for them, and re-layouts  1.62 us

profile of v3, /device:TPU:26, one launch (start us, length us, event | category | flops | bytes accessed | tf_op | source)
XLA Modules:
  0.0 23.7 jit_solution(7014613298244455659)
XLA Ops:
  0.0 22.1 %multilevel.1 = f32[48,8,128]{2,1,0:T(8,128)} custom-call(f32[48,8,128]{2,1,0:T(8,128)} %charge_hbm.1, f32[11,11,11]{2,1,0:T(8,128)} %kernel_fine_hbm.1, f32[11,11,11]{2,1,0:T(8,128)} %kernel_mid_hbm.1, f32[11,11,11]{2,1,0:T(8,128)} %kernel_top_hbm.1), custom_call_target="tpu_custom_call" | custom-call | tf_op jit(solution)/shard_map/multilevel/pallas_call | solution.py:377
  22.1 1.6 %copy.6 = f32[48,8,128]{2,1,0:T(8,128)} copy(f32[48,8,128]{2,1,0:T(8,128)} %multilevel.1) | data formatting | bytes 393216

commit v4 on v3

--- a/solution.py
+++ b/solution.py
@@ -16,7 +16,6 @@
 
 FX, FROW = 6, 8
 MX, TX = 6, 6
-REACH = 4
 
 
 def messages():
@@ -222,6 +221,7 @@
     padded, rows_f, rows_m, rows_t,
     wfh, wfl, wmh, wml, wth, wtl, afh, afl, amh, aml, ath, atl,
     total, pot_z, pot_y, top_z, top_y, load_sems, send_sems, recv_sems,
+    near_sem, far_sem,
 ):
     gx, gy = lax.axis_index("gx"), lax.axis_index("gy")
 
@@ -273,17 +273,25 @@
     for ref in (fine, middle, top):
         ref[...] = jnp.zeros_like(ref)
 
+    def greet(semaphore, reach):
+        for dx in (-1, 0, 1):
+            for dy in range(-reach, reach + 1):
+                if dx == 0 and dy == 0:
+                    continue
+                @pl.when(exists(dx, dy))
+                def _(dx=dx, dy=dy):
+                    pl.semaphore_signal(
+                        semaphore, inc=1, device_id={"gx": gx + dx, "gy": gy + dy},
+                        device_id_type=pl.DeviceIdType.MESH,
+                    )
+
+    def greeted(semaphore, reach):
+        across = 1 + (gx > 0).astype(jnp.int32) + (gx < nx - 1).astype(jnp.int32)
+        along = 1 + jnp.minimum(gy, reach) + jnp.minimum(ny - 1 - gy, reach)
+        pl.semaphore_wait(semaphore, across * along - 1)
+
     barrier = pltpu.get_barrier_semaphore()
-    for dx in (-1, 0, 1):
-        for dy in range(-REACH, REACH + 1):
-            if dx == 0 and dy == 0:
-                continue
-            @pl.when(exists(dx, dy))
-            def _(dx=dx, dy=dy):
-                pl.semaphore_signal(
-                    barrier, inc=1, device_id={"gx": gx + dx, "gy": gy + dy},
-                    device_id_type=pl.DeviceIdType.MESH,
-                )
+    greet(barrier, 1)
 
     for ref in (along_fine, along_middle):
         ref[...] = jnp.zeros_like(ref)
@@ -293,34 +301,36 @@
     fine[FX : FX + 48, FROW : FROW + 8, :] = charge[...]
     base_rows(kernel_mid, padded, rows_m, 64)
     toeplitz(rows_m, wmh, wml, 64, 768, 2)
+    base_rows(kernel_fine, padded, rows_f, 128)
+
+    greeted(barrier, 1)
+    start(range(N_FINE))
+    greet(near_sem, 1)
+    toeplitz(rows_f, wfh, wfl, 128, 1408, 5)
+    greeted(near_sem, 1)
+    greet(far_sem, 2)
     base_rows(kernel_top, padded, rows_t, 32)
     toeplitz(rows_t, wth, wtl, 32, 384, 1)
-    base_rows(kernel_fine, padded, rows_f, 128)
-
-    across = 1 + (gx > 0).astype(jnp.int32) + (gx < nx - 1).astype(jnp.int32)
-    along = 1 + jnp.minimum(gy, REACH) + jnp.minimum(ny - 1 - gy, REACH)
-    pl.semaphore_wait(barrier, across * along - 1)
-
-    start(range(N_FINE))
-    toeplitz(rows_f, wfh, wfl, 128, 1408, 5)
     arrive(range(N_FINE))
 
     near = restrict(fine, along_fine, 0, 2, 0, 128)
     near = jnp.where(inside(27, gx * 24 - 2, nx * 24, gy * 4 - 2, ny * 4, 64), near, 0.0)
     middle[MX : MX + 24, 8:12, :] = near[2:26, 2:6, :]
     top[TX : TX + 12, 8:10, :] = restrict(near, along_middle, 0, 8, 8, 64)[:, 0:2, :]
-    start(range(N_FINE, COUNT))
+    start(range(N_FINE, N_MIDDLE))
+    greeted(far_sem, 2)
+    start(range(N_MIDDLE, COUNT))
 
     gather_taps(fine, afh, afl, 1, 3, 128)
     total[...] = jnp.zeros_like(total)
 
-    for i in range(3):
+    for i in range(2):
         fine_step(i, afh, afl, wfh, wfl, total)
 
-    arrive(range(N_FINE, N_MIDDLE))
+    arrive(range(N_FINE, COUNT))
     gather_taps(middle, amh, aml, 0, 2, 64)
-    arrive(range(N_MIDDLE, COUNT))
     gather_taps(top, ath, atl, 0, 2, 32)
+    fine_step(2, afh, afl, wfh, wfl, total)
     top_pot = small_convolution(ath, atl, wth, wtl, 11, 4, 2, 384, 32, 15)
     top_pot = jnp.where(inside(15, gx * 12 - 1, nx * 12, gy * 2 - 1, ny * 2, 32), top_pot, 0.0)
     top_z[...] = exact_dot(top_pot.reshape(120, 32), prolong_matrix(32)).reshape(15, 8, 64)
@@ -371,6 +381,7 @@
         vmem((15, 8, 64), F32), vmem((15, 8, 64), F32),
         pltpu.SemaphoreType.DMA((4,)),
         pltpu.SemaphoreType.DMA((COUNT,)), pltpu.SemaphoreType.DMA((COUNT,)),
+        pltpu.SemaphoreType.REGULAR, pltpu.SemaphoreType.REGULAR,
     ]
 
     def shards(charge, kernel_fine, kernel_mid, kernel_top):

time: 24.1 us -> 23.2 us (0.963)
  Pallas kernels: 22.1 us -> 21.3 us
    pallas_call x1, Pallas kernels: 22.1 us -> 21.3 us  [shards(): pl.pallas_call(functools.partial(whole, nx, ny), out_shape=jax.ShapeDtype...]
where the time goes in v4:
time: 23.2 us; the launch traced here: 23 us
  Pallas kernels  21.3 us (92%)
  local copies, waits for them, and re-layouts  1.62 us (7%)
    pallas_call x1, Pallas kernels, shards(): pl.pallas_call(functools.partial(whole, nx, ny), out_shape=jax.ShapeDtype...  21.3 us
    unnamed x1, local copies, waits for them, and re-layouts  1.62 us

profile of v4, /device:TPU:26, one launch (start us, length us, event | category | flops | bytes accessed | tf_op | source)
XLA Modules:
  0.0 23.0 jit_solution(4709563735874821758)
XLA Ops:
  0.0 21.3 %multilevel.1 = f32[48,8,128]{2,1,0:T(8,128)} custom-call(f32[48,8,128]{2,1,0:T(8,128)} %charge_hbm.1, f32[11,11,11]{2,1,0:T(8,128)} %kernel_fine_hbm.1, f32[11,11,11]{2,1,0:T(8,128)} %kernel_mid_hbm.1, f32[11,11,11]{2,1,0:T(8,128)} %kernel_top_hbm.1), custom_call_target="tpu_custom_call" | custom-call | tf_op jit(solution)/shard_map/multilevel/pallas_call | solution.py:388
  21.3 1.6 %copy.6 = f32[48,8,128]{2,1,0:T(8,128)} copy(f32[48,8,128]{2,1,0:T(8,128)} %multilevel.1) | data formatting | bytes 393216

commit v5 on v4

--- a/solution.py
+++ b/solution.py
@@ -15,7 +15,7 @@
 RADIUS = 5
 
 FX, FROW = 6, 8
-MX, TX = 6, 6
+MX, TX = 3, 2
 
 
 def messages():
@@ -27,14 +27,14 @@
             sy = {1: (2, 6), 0: (0, 8), -1: (0, 5)}[dy]
             ty = {1: 2, 0: 8, -1: 16}[dy]
             fine.append((dx, dy, sx, sy, tx, ty))
-        sx = {1: (24, 6), 0: (6, 24), -1: (6, 6)}[dx]
-        tx = {1: 0, 0: 6, -1: 30}[dx]
+        sx = {1: (12, 3), 0: (3, 12), -1: (3, 3)}[dx]
+        tx = {1: 0, 0: 3, -1: 15}[dx]
         for dy in range(-2, 3):
             sy = {2: (10, 2), -2: (8, 2)}.get(dy, (8, 4))
             ty = {2: 2, 1: 4, 0: 8, -1: 12, -2: 16}[dy]
             middle.append((dx, dy, sx, sy, tx, ty))
-        sx = {1: (12, 6), 0: (6, 12), -1: (6, 7)}[dx]
-        tx = {1: 0, 0: 6, -1: 18}[dx]
+        sx = {1: (3, 2), 0: (2, 3), -1: (2, 2)}[dx]
+        tx = {1: 0, 0: 2, -1: 5}[dx]
         for dy in range(-4, 4):
             top.append((dx, dy, sx, (8, 2), tx, 8 - 2 * dy))
     return [[m for m in group if m[:2] != (0, 0)] for group in (fine, middle, top)]
@@ -124,23 +124,28 @@
         group(i)
 
 
+def pack(planes, z):
+    per = 128 // z
+    groups = [
+        jnp.concatenate([planes[per * g + q] for q in range(per)], axis=-1)[None]
+        for g in range(planes.shape[0] // per)
+    ]
+    return jnp.concatenate(groups, axis=0)
+
+
 def gather_taps(window, high_ref, low_ref, first_plane, first_row, z):
     per = 128 // z
-
-    def pair(p):
+    for p in range(high_ref.shape[0]):
         for lane_block in range(high_ref.shape[2] // 128):
-            pieces = []
-            for q in range(per):
-                row = first_row + lane_block * per + q
-                pieces.append(window[pl.ds(first_plane + 2 * p, 2), row : row + 8, :])
-            value = pieces[0] if per == 1 else jnp.concatenate(pieces, axis=-1)
-            high, low = split(value.reshape(16, 128))
+            planes = []
+            for plane in (first_plane + 2 * p, first_plane + 2 * p + 1):
+                row, at = first_row + lane_block * per, plane % per * z
+                pieces = [window[plane // per, row + q : row + q + 8, at : at + z] for q in range(per)]
+                planes.append(pieces[0] if per == 1 else jnp.concatenate(pieces, axis=-1))
+            high, low = split(jnp.concatenate(planes, axis=0))
             at = slice(lane_block * 128, lane_block * 128 + 128)
             high_ref[p, :, at] = high
             low_ref[p, :, at] = low
-
-    for p in range(high_ref.shape[0]):
-        pair(p)
 
 
 def products(ah, al, wh, wl):
@@ -315,8 +320,8 @@
 
     near = restrict(fine, along_fine, 0, 2, 0, 128)
     near = jnp.where(inside(27, gx * 24 - 2, nx * 24, gy * 4 - 2, ny * 4, 64), near, 0.0)
-    middle[MX : MX + 24, 8:12, :] = near[2:26, 2:6, :]
-    top[TX : TX + 12, 8:10, :] = restrict(near, along_middle, 0, 8, 8, 64)[:, 0:2, :]
+    middle[MX : MX + 12, 8:12, :] = pack(near[2:26], 64)[:, 2:6, :]
+    top[TX : TX + 3, 8:10, :] = pack(restrict(near, along_middle, 0, 8, 8, 64), 32)[:, 0:2, :]
     start(range(N_FINE, N_MIDDLE))
     greeted(far_sem, 2)
     start(range(N_MIDDLE, COUNT))
@@ -329,7 +334,7 @@
 
     arrive(range(N_FINE, COUNT))
     gather_taps(middle, amh, aml, 0, 2, 64)
-    gather_taps(top, ath, atl, 0, 2, 32)
+    gather_taps(top, ath, atl, 2, 2, 32)
     fine_step(2, afh, afl, wfh, wfl, total)
     top_pot = small_convolution(ath, atl, wth, wtl, 11, 4, 2, 384, 32, 15)
     top_pot = jnp.where(inside(15, gx * 12 - 1, nx * 12, gy * 2 - 1, ny * 2, 32), top_pot, 0.0)
@@ -370,8 +375,8 @@
     scratch = [
         vmem((48, 8, 128), F32), vmem((11, 11, 11), F32), vmem((11, 11, 11), F32),
         vmem((11, 11, 11), F32),
-        vmem((62, 24, 128), F32), vmem((27, 32, 128), F32), vmem((40, 24, 64), F32),
-        vmem((12, 32, 64), F32), vmem((32, 24, 32), F32), vmem((16, 16, 128), F32),
+        vmem((62, 24, 128), F32), vmem((27, 32, 128), F32), vmem((20, 24, 128), F32),
+        vmem((12, 32, 64), F32), vmem((8, 24, 128), F32), vmem((16, 16, 128), F32),
         vmem((12, 16, 128), F32), vmem((6, 16, 128), F32), vmem((4, 16, 128), F32),
         vmem((8448, 256), BF), vmem((8448, 256), BF), vmem((2304, 256), BF), vmem((2304, 256), BF),
         vmem((768, 256), BF), vmem((768, 256), BF),

time: 23.2 us -> 21.9 us (0.944)
  the two profiles are of different devices: /device:TPU:26 before, /device:TPU:25 now
where the time goes in v5:
time: 21.9 us; the launch traced here: 21.7 us
  Pallas kernels  20.1 us (92%)
  local copies, waits for them, and re-layouts  1.62 us (7%)
    pallas_call x1, Pallas kernels, shards(): pl.pallas_call(functools.partial(whole, nx, ny), out_shape=jax.ShapeDtype...  20.1 us
    unnamed x1, local copies, waits for them, and re-layouts  1.62 us

profile of v5, /device:TPU:25, one launch (start us, length us, event | category | flops | bytes accessed | tf_op | source)
XLA Modules:
  0.0 21.7 jit_solution(10673817382826969328)
XLA Ops:
  0.0 20.1 %multilevel.1 = f32[48,8,128]{2,1,0:T(8,128)} custom-call(f32[48,8,128]{2,1,0:T(8,128)} %charge_hbm.1, f32[11,11,11]{2,1,0:T(8,128)} %kernel_fine_hbm.1, f32[11,11,11]{2,1,0:T(8,128)} %kernel_mid_hbm.1, f32[11,11,11]{2,1,0:T(8,128)} %kernel_top_hbm.1), custom_call_target="tpu_custom_call" | custom-call | tf_op jit(solution)/shard_map/multilevel/pallas_call | solution.py:393
  20.1 1.6 %copy.6 = f32[48,8,128]{2,1,0:T(8,128)} copy(f32[48,8,128]{2,1,0:T(8,128)} %multilevel.1) | data formatting | bytes 393216
